TPU v7x, 32 devices: a whole 2x2x4 slice. The times are simulated.
32 devices in a mesh: group: 2 (over y), wide: 4 (over z), sub: 2 (over x), pol: 2 (over core).
Axes of the slice: x: 2, y: 2, z: 4, core: 2. Of those that a mesh axis runs over, the one named last changes fastest.
Arguments:
- voltages: bfloat16 [2, 2048, 4, 2048], P('pol', ('group', 'wide'), 'sub'), parts along dimension 1, may hold values from -6 to 6
- real_weight: bfloat16 [512, 1024, 256], P(('wide', 'sub', 'pol')), may hold values from -0.125 to 0.125
- imaginary_weight: bfloat16 [512, 1024, 256], P(('wide', 'sub', 'pol')), may hold values from -0.125 to 0.125
- delays: int32 [128, 512], P('pol'), may hold values from 0 to 3
Outputs:
- dedispersed: float32 [512, 4, 128], P(('group', 'wide', 'sub'), None, 'pol'), parts along dimension 0
There are 2 independent parts, one for each index of `group`. A program takes and returns all parts, laid end to end along the dimension named above; an argument that names none is the same for every part. Nothing has to cross between parts.
Inputs may be any that keep to these rules, and one draw needn't show every extreme that they name: `delays`: integer sample shifts of each delay trial and channel.
All inputs are finite; a program needn't handle non-finite values.
Results may differ from a plain program's by a relative error of at most 0.012.
Values may be sent and summed in bfloat16 or wider, within the bound.
A program may use at most 256 MiB of HBM per device.

v0:
```python
import math

import jax
import jax.numpy as jnp
from jax import lax
from jax.sharding import PartitionSpec as P


def dft_table(sample_total, channel_total):
    first_bin = sample_total // 2 - channel_total
    freq_bins = first_bin + jnp.arange(channel_total, dtype=jnp.int32)
    sample_ids = jnp.arange(sample_total, dtype=jnp.int32)
    turns = freq_bins[:, None] * sample_ids[None, :] % sample_total
    angles = turns.astype(jnp.float32) * (2.0 * math.pi / sample_total)
    factor = 1.0 / math.sqrt(sample_total)
    exact = jnp.stack([jnp.cos(angles) * factor, -jnp.sin(angles) * factor], axis=1)
    upper = exact.astype(jnp.bfloat16)
    lower = (exact - upper.astype(jnp.float32)).astype(jnp.bfloat16)
    return jnp.stack([upper, lower], axis=2).reshape(4 * channel_total, sample_total)


def voltage_turn(blocks_in):
    result = lax.all_to_all(blocks_in, ("wide", "sub"), split_axis=0, concat_axis=0, tiled=True)
    return result


def pol_turn(blocks_in):
    return lax.all_to_all(blocks_in, "pol", split_axis=1, concat_axis=1, tiled=True)


def power_turn(blocks_in):
    result = lax.all_to_all(blocks_in, ("wide", "sub"), split_axis=0, concat_axis=0, tiled=True)
    return result


def dedisperse(power_all, delay_rows, frames, channel_total):
    frame_ids = jnp.arange(frames, dtype=jnp.int32)
    scale_step = 2.0 * math.pi / frames
    fwd_angle = (frame_ids[:, None] * frame_ids[None, :] % frames).astype(jnp.float32) * scale_step
    keeper = (frame_ids != 0).astype(jnp.float32)[:, None]
    fwd_cos = jnp.cos(fwd_angle) * keeper
    fwd_sin = jnp.sin(fwd_angle) * keeper
    spec_re = jnp.einsum("kn,cnb->kcb", fwd_cos, power_all, precision=lax.Precision.HIGHEST)
    spec_im = -jnp.einsum("kn,cnb->kcb", fwd_sin, power_all, precision=lax.Precision.HIGHEST)
    block = 8 if frames % 8 == 0 else frames
    beam_local = power_all.shape[2]
    trial_local = delay_rows.shape[0]

    def add_block(step_index, total):
        start = step_index * block
        freq_vals = start + jnp.arange(block, dtype=jnp.int32)
        turns = freq_vals[:, None, None] * delay_rows[None, :, :] % frames
        angles = turns.astype(jnp.float32) * scale_step
        rot_cos = jnp.cos(angles)
        rot_sin = jnp.sin(angles)
        part_re = lax.dynamic_slice_in_dim(spec_re, start, block, 0)
        part_im = lax.dynamic_slice_in_dim(spec_im, start, block, 0)
        sum_re = jnp.einsum(
            "ktc,kcb->ktb", rot_cos, part_re, precision=lax.Precision.HIGHEST
        ) - jnp.einsum("ktc,kcb->ktb", rot_sin, part_im, precision=lax.Precision.HIGHEST)
        sum_im = jnp.einsum(
            "ktc,kcb->ktb", rot_sin, part_re, precision=lax.Precision.HIGHEST
        ) + jnp.einsum("ktc,kcb->ktb", rot_cos, part_im, precision=lax.Precision.HIGHEST)
        back_angle = (freq_vals[:, None] * frame_ids[None, :] % frames).astype(
            jnp.float32
        ) * scale_step
        total = total + jnp.einsum(
            "ktb,kn->bnt", sum_re, jnp.cos(back_angle), precision=lax.Precision.HIGHEST
        )
        return total - jnp.einsum(
            "ktb,kn->bnt", sum_im, jnp.sin(back_angle), precision=lax.Precision.HIGHEST
        )

    initial = jnp.zeros((beam_local, frames, trial_local), jnp.float32)
    total = lax.fori_loop(0, frames // block, add_block, initial)
    return total * (1.0 / (frames * math.sqrt(channel_total)))


def local(voltages, real_weight, imaginary_weight, delays):
    widening_count = lax.axis_size("wide")
    subband_count = lax.axis_size("sub")
    polar_count = lax.axis_size("pol")
    group_list = widening_count * subband_count
    antenna_slice = voltages.shape[1]
    frame_slice = voltages.shape[2]
    sample_total = voltages.shape[3]
    channel_pairs = real_weight.shape[0]
    beam_total = real_weight.shape[2]
    channel_total = channel_pairs * group_list * polar_count
    frames = subband_count * frame_slice
    sample_matrix = voltages[0].reshape(antenna_slice * frame_slice, sample_total)
    dft_weights = dft_table(sample_total, channel_total)
    weighted_product = lax.dot_general(
        dft_weights, sample_matrix, (((1,), (1,)), ((), ())), preferred_element_type=jnp.float32
    )
    spectrum_rows = (
        weighted_product.reshape(channel_total, 2, 2, antenna_slice * frame_slice)
        .sum(axis=2)
        .astype(jnp.bfloat16)
    )
    current_blocks = spectrum_rows.reshape(
        group_list, polar_count, channel_pairs * 2, antenna_slice * frame_slice
    )
    current_blocks = pol_turn(voltage_turn(current_blocks))
    voltage_collection = current_blocks.reshape(
        widening_count, subband_count, polar_count, channel_pairs, 2, antenna_slice, frame_slice
    )
    real_section = real_weight.reshape(channel_pairs, widening_count, antenna_slice, beam_total)
    imaginary_split = imaginary_weight.reshape(
        channel_pairs, widening_count, antenna_slice, beam_total
    )
    form_re = jnp.stack([real_section, -imaginary_split], axis=1)
    form_im = jnp.stack([imaginary_split, real_section], axis=1)
    real_form = jnp.stack([form_re, form_im], axis=4)
    beam_field = jnp.einsum(
        "wsqckaf,ckwaob->cqsfob", voltage_collection, real_form, preferred_element_type=jnp.float32
    )
    power_field = jnp.sum(beam_field * beam_field, axis=(1, 4)).reshape(
        channel_pairs, frames, beam_total
    )
    beam_local = beam_total // group_list
    outgoing = power_field.reshape(channel_pairs, frames, group_list, beam_local)
    outgoing = jnp.transpose(outgoing, (2, 0, 1, 3)).reshape(
        group_list, channel_pairs * frames * beam_local
    )
    arrived = power_turn(outgoing)
    both_pols = lax.all_gather(
        arrived.reshape(group_list, 1, channel_pairs * frames * beam_local),
        "pol",
        axis=1,
        tiled=True,
    )
    power_all = both_pols.reshape(channel_total, frames, beam_local)
    return dedisperse(power_all, delays, frames, channel_total)


def solution(mesh):
    placed = (
        P("pol", ("group", "wide"), "sub", None),
        P(("wide", "sub", "pol"), None, None),
        P(("wide", "sub", "pol"), None, None),
        P("pol", None),
    )
    return jax.shard_map(
        local,
        mesh=mesh,
        in_specs=placed,
        out_specs=P(("group", "wide", "sub"), None, "pol"),
        check_vma=False,
    )
```

profile of v0, /device:TPU:0, one launch (start us, length us, event | category | flops | bytes accessed | tf_op | source)
XLA Modules:
  0.0 323.3 jit_solution(8248861408916826605)
XLA Ops:
  0.0 16.9 %multiply_bitcast_fusion.1 = (f32[512,1,1,2048]{3,0,2,1:T(8,128)S(1)}, f32[512,1,1,2048]{3,0,2,1:T(8,128)S(1)}) fusion(s32[512]{0:T(512)S(1)} %iota_add_fusion), kind=kLoop, calls=%fused_computation.21 | loop fusion | flops 17825792 | bytes 8390656 | tf_op jit(solution)/shard_map/stack | solution.py:16
  16.9 2.4 subtract_convert_fusion
  19.3 2.7 fusion.8
  22.0 2.2 reshape.211
  24.2 8.7 %fusion.16 = bf16[512,2,512]{2,0,1:T(8,128)(2,1)S(1)} fusion(bf16[512,2048,1,1]{1,0,2,3:T(8,128)(2,1)} %reshape.211, bf16[512,2,1,2048]{3,0,2,1:T(8,128)(2,1)} %subtract_convert_fusion, bf16[512,2,1,2048]{3,0,2,1:T(8,128)(2,1)} %fusion.8), kind=kOutput, calls=%fused_computation.26 | convolution fusion | flops 4299685888 | bytes 11534336 | tf_op jit(solution)/shard_map/dot_general | solution.py:93
  32.9 1.1 copy.55
  34.0 1.2 convert_element_type.107
  35.2 7.3 %all-to-all-start = ((bf16[8,2,64,512]{3,2,1,0:T(8,128)(2,1)}), bf16[8,2,64,512]{3,2,1,0:T(8,128)(2,1)S(1)}, u32[]{:S(2)}, u32[]{:S(2)}) async-start(bf16[8,2,64,512]{3,2,1,0:T(8,128)(2,1)} %convert_element_type.107), calls=%async_computation | async-start | bytes 2097152 | tf_op jit(solution)/shard_map/all_to_all | solution.py:23
  42.5 14.7 %neg.32 = bf16[32,1,4,256,256]{4,3,2,1,0:T(8,128)(2,1)} negate(bf16[32,1,4,256,256]{4,3,2,1,0:T(8,128)(2,1)} %bitcast.74) | non-fusion elementwise | flops 8388608 | bytes 33554432 | tf_op jit(solution)/shard_map/neg | solution.py:112
  57.2 44.1 %maximum_bitcast_fusion.2 = (bf16[32,2,4,256,1,256]{5,3,2,1,4,0:T(8,128)(2,1)}, bf16[32,2,4,256,1,256]{5,3,2,1,4,0:T(8,128)(2,1)}) fusion(bf16[32,1,4,256,256]{4,3,2,1,0:T(8,128)(2,1)} %neg.32, bf16[32,1,4,256,256]{4,3,2,1,0:T(8,128)(2,1)} %bitcast.76, bf16[32,1,4,256,256]{4,3,2,1,0:T(8,128)(2,1)} %bitcast.75), kind=kLoop, calls=%fused_computation.5 | loop fusion | flops 33554432 | bytes 117440512 | tf_op jit(solution)/shard_map/stack | solution.py:114
  101.4 4.6 %all_to_all.20 = bf16[8,2,64,512]{3,2,0,1:T(8,128)(2,1)S(1)} all-to-all(bf16[8,2,64,512]{3,2,0,1:T(8,128)(2,1)S(1)} %copy.56), channel_id=1, replica_groups=mesh['group'=2,'wide'=4,'sub'=2,'pol'=2] {'pol'}, dimensions={1} | all-to-all | bytes 2097152 | tf_op jit(solution)/shard_map/all_to_all | solution.py:28
  106.0 145.5 %reshape.220 = bf16[4,2,2,32,2,256,2]{6,5,4,3,1,0,2:T(8,128)(2,1)} reshape(bf16[8,2,64,512]{3,2,0,1:T(8,128)(2,1)S(1)} %all_to_all.20) | data formatting | bytes 2097152 | tf_op jit(solution)/shard_map/reshape | solution.py:105
  251.5 42.6 %fusion.27 = f32[32,256,2,2]{1,3,2,0:T(2,128)S(1)} fusion(bf16[32,2,4,256,1,256]{5,3,2,1,4,0:T(8,128)(2,1)} %get-tuple-element.18, bf16[32,2,4,256,1,256]{5,3,2,1,4,0:T(8,128)(2,1)} %get-tuple-element.17, bf16[4,2,2,32,2,256,2]{6,5,4,3,1,0,2:T(8,128)(2,1)} %reshape.220), kind=kOutput, calls=%fused_computation.29 | convolution fusion | flops 671318016 | bytes 68288512 | tf_op jit(solution)/shard_map/wsqckaf,ckwaob->cqsfob/dot_general | solution.py:115
  294.7 1.0 all_to_all.16
  295.7 6.0 %all-to-all-start.2 = ((f32[8,1,4096]{2,1,0:T(1,128)}), f32[8,1,4096]{2,1,0:T(1,128)S(1)}, u32[]{:S(2)}, u32[]{:S(2)}) async-start(f32[8,1,4096]{2,1,0:T(1,128)} %all_to_all.16), calls=%async_computation.2 | async-start | bytes 262144 | tf_op jit(solution)/shard_map/all_to_all | solution.py:32
  301.7 7.3 %all-to-all-done.2 = f32[8,1,4096]{2,1,0:T(1,128)S(1)} async-done(((f32[8,1,4096]{2,1,0:T(1,128)}), f32[8,1,4096]{2,1,0:T(1,128)S(1)}, u32[]{:S(2)}, u32[]{:S(2)}) %all-to-all-start.2) | async-done | bytes 131104 | tf_op jit(solution)/shard_map/all_to_all | solution.py:32
  309.1 2.2 all_gather.3
  312.5 0.7 fusion.57
  313.3 0.7 fusion.55
  314.0 2.0 fusion.41
  316.0 2.0 fusion.43
  318.0 2.0 convolution_subtract_fusion.1
  320.3 2.0 convolution_add_fusion
  322.3 1.0 fusion.31
  (16 shorter events, 2.2 us)
Async XLA Ops:
  19.3 2.7 copy-start
  35.2 66.1 %all-to-all-start = ((bf16[8,2,64,512]{3,2,1,0:T(8,128)(2,1)}), bf16[8,2,64,512]{3,2,1,0:T(8,128)(2,1)S(1)}, u32[]{:S(2)}, u32[]{:S(2)}) async-start(bf16[8,2,64,512]{3,2,1,0:T(8,128)(2,1)} %convert_element_type.107), calls=%async_computation | async-start | bytes 2097152 | tf_op jit(solution)/shard_map/all_to_all | solution.py:23
  294.1 19.9 %copy-start.1 = (s32[64,512]{1,0:T(8,128)S(1)}, s32[64,512]{1,0:T(8,128)}, u32[]{:S(2)}) copy-start(s32[64,512]{1,0:T(8,128)} %param.7) | copy-start | bytes 393220
  295.7 13.3 %all-to-all-start.2 = ((f32[8,1,4096]{2,1,0:T(1,128)}), f32[8,1,4096]{2,1,0:T(1,128)S(1)}, u32[]{:S(2)}, u32[]{:S(2)}) async-start(f32[8,1,4096]{2,1,0:T(1,128)} %all_to_all.16), calls=%async_computation.2 | async-start | bytes 262144 | tf_op jit(solution)/shard_map/all_to_all | solution.py:32
where the time goes:
time: 324 us; the launch traced here: 323 us
  local copies, waits for them, and re-layouts  153 us (47%)
  other arithmetic  80.8 us (25%)
  matrix products  62 us (19%)
  starting transfers between devices  13.3 us (4%)
  waiting for transfers between devices  7.34 us (2%)
  blocking collectives  6.79 us (2%)
    reshape x1, local copies, waits for them, and re-layouts, local(): current_blocks.reshape(widening_count, subband_count, polar_count, channe...  146 us
    another operation x1, other arithmetic, local(): real_form = jnp.stack([form_re, form_im], axis=4)  44.1 us
    dot_general x1, matrix products, local(): jnp.einsum('wsqckaf,ckwaob->cqsfob', voltage_collection, real_form, prefe...  42.6 us
    another operation x1, other arithmetic, dft_table(): jnp.stack([jnp.cos(angles) * factor, -jnp.sin(angles) * factor], axis=1)  16.9 us
    neg x1, other arithmetic, local(): form_re = jnp.stack([real_section, -imaginary_split], axis=1)  14.7 us
    dot_general x1, matrix products, local(): lax.dot_general(dft_weights, sample_matrix, (((1,), (1,)), ((), ())), pre...  8.67 us
    all_to_all x1, waiting for transfers between devices, power_turn(): lax.all_to_all(blocks_in, ('wide', 'sub'), split_axis=0, concat_axis=0, t...  7.34 us
    all_to_all x1, starting transfers between devices, voltage_turn(): lax.all_to_all(blocks_in, ('wide', 'sub'), split_axis=0, concat_axis=0, t...  7.28 us
  transfers between devices with their start and end apart: 2, of which 1 were waited for; matrix products, arithmetic and copies ran while one was open for 18% of the time, Pallas kernels for 0%

commit v1 on v0

--- a/solution.py
+++ b/solution.py
@@ -1,8 +1,12 @@
+import functools
 import math
 
 import jax
 import jax.numpy as jnp
+import numpy as np
 from jax import lax
+from jax.experimental import pallas as pl
+from jax.experimental.pallas import tpu as pltpu
 from jax.sharding import PartitionSpec as P
 
 
@@ -76,7 +80,7 @@
     return total * (1.0 / (frames * math.sqrt(channel_total)))
 
 
-def local(voltages, real_weight, imaginary_weight, delays):
+def staged_local(voltages, real_weight, imaginary_weight, delays):
     widening_count = lax.axis_size("wide")
     subband_count = lax.axis_size("sub")
     polar_count = lax.axis_size("pol")
@@ -134,6 +138,287 @@
     return dedisperse(power_all, delays, frames, channel_total)
 
 
+MESH = pl.DeviceIdType.MESH
+
+
+def flip(index, mask, size):
+    out, bit = 0, 1
+    while bit < size:
+        own = (index // bit) % 2
+        out = out + bit * ((1 - own) if (mask // bit) % 2 else own)
+        bit *= 2
+    return out
+
+
+def window_kernel(
+    dims, v_ref, wr_hbm, wi_hbm, d_ref, cb_ref, sb_ref, ca_ref, sa_ref, out_ref,
+    wr, wi, table, sent, held, acc, power, outgoing, arrived, hot,
+    w_sem, send_sem, recv_sem, own_sem, psend_sem, precv_sem,
+):
+    wides, subs, pols, fslice = dims
+    per_wide = subs * pols
+    owners = wides * per_wide
+    antennas = v_ref.shape[1]
+    samples = v_ref.shape[2]
+    channels = wr.shape[0]
+    beams = wr.shape[2]
+    frames = subs * fslice
+    trials, channel_total = d_ref.shape
+    rows = 2 * channels
+    beam_local = outgoing.shape[1]
+    lanes = 128
+    w, s, q = lax.axis_index("wide"), lax.axis_index("sub"), lax.axis_index("pol")
+
+    def place(m):
+        mw, ms, mq = m // per_wide, (m // pols) % subs, m % pols
+        return flip(w, mw, wides), flip(s, ms, subs), flip(q, mq, pols)
+
+    def ident(m):
+        tw, ts, tq = place(m)
+        return {"wide": tw, "sub": ts, "pol": tq}
+
+    barrier = pltpu.get_barrier_semaphore()
+    for m in range(1, owners):
+        pl.semaphore_signal(barrier, inc=1, device_id=ident(m), device_id_type=MESH)
+
+    loads = []
+    for mw in range(wides):
+        tw = flip(w, mw, wides)
+        part = pl.ds(pl.multiple_of(tw * antennas, antennas), antennas)
+        pair = []
+        for k, (src, dst) in enumerate(((wr_hbm, wr), (wi_hbm, wi))):
+            copy = pltpu.make_async_copy(src.at[:, part, :], dst.at[:, part, :], w_sem.at[mw, k])
+            copy.start()
+            pair.append(copy)
+        loads.append(pair)
+
+    chunk = per_wide * rows
+    cycle = ca_ref.shape[1]
+    copies = [None] * owners
+    for j in range(wides):
+        mw = wides - 1 - j
+        tw = flip(w, mw, wides)
+        base = pl.multiple_of(tw * chunk, chunk)
+
+        def fill(n1, carry, base=base):
+            cos_in = cb_ref[pl.ds(base, chunk), :].reshape(chunk // cycle, cycle, lanes)
+            sin_in = sb_ref[pl.ds(base, chunk), :].reshape(chunk // cycle, cycle, lanes)
+            value = cos_in * ca_ref[n1][None] - sin_in * sa_ref[n1][None]
+            table[:, pl.ds(pl.multiple_of(n1 * lanes, lanes), lanes)] = value.reshape(chunk, lanes).astype(jnp.bfloat16)
+            return carry
+
+        lax.fori_loop(0, samples // lanes, fill, 0)
+        for f in range(fslice):
+            spectrum = lax.dot_general(
+                table[...], v_ref[f], (((1,), (1,)), ((), ())), preferred_element_type=jnp.float32
+            )
+            sent[j, f] = spectrum.astype(jnp.bfloat16)
+        if j == 0:
+            pl.semaphore_wait(barrier, owners - 1)
+        for r in reversed(range(per_wide)):
+            m = mw * per_wide + r
+            tw, ts, tq = place(m)
+            part = pl.ds(pl.multiple_of((ts * pols + tq) * rows, rows), rows)
+            source = sent.at[j, :, part, :]
+            target = held.at[w, q * subs + s]
+            if m == 0:
+                copy = pltpu.make_async_copy(source, target, own_sem.at[0])
+            else:
+                copy = pltpu.make_async_remote_copy(
+                    src_ref=source, dst_ref=target, send_sem=send_sem.at[m], recv_sem=recv_sem.at[m],
+                    device_id=ident(m), device_id_type=MESH,
+                )
+            copy.start()
+            copies[m] = copy
+
+    per_tile = lanes // channels
+    lane = lax.broadcasted_iota(jnp.int32, (lanes, lanes), 1)
+    line = lax.broadcasted_iota(jnp.int32, (lanes, lanes), 0)
+    frame_lane = lax.broadcasted_iota(jnp.int32, (trials, lanes), 1) // channels
+    for i in range(per_tile):
+        spread = (line == i * channels + lane % channels).astype(jnp.float32).astype(jnp.bfloat16)
+        for t in range(channel_total // lanes):
+            wrapped = (d_ref[:, t * lanes:(t + 1) * lanes] & (frames - 1)).astype(jnp.float32).astype(jnp.bfloat16)
+            wide_delay = jnp.dot(wrapped, spread, preferred_element_type=jnp.float32)
+            at = (t * per_tile + i) * lanes
+            for n in range(frames):
+                wanted = ((frame_lane - n) & (frames - 1)).astype(jnp.float32)
+                hot[n * trials:(n + 1) * trials, at:at + lanes] = (wide_delay == wanted).astype(jnp.float32).astype(jnp.bfloat16)
+
+    tile = 16
+    group = tile // 2
+    parts = per_wide * fslice
+    member = lax.broadcasted_iota(jnp.int32, (parts * tile, antennas), 0) // 2 % group
+    for mw in range(wides):
+        tw = flip(w, mw, wides)
+        for copy in loads[mw]:
+            copy.wait()
+        for r in range(per_wide):
+            m = mw * per_wide + r
+            if m == 0:
+                copies[0].wait()
+            else:
+                copies[m].wait_recv()
+        span = pl.ds(pl.multiple_of(tw * antennas, antennas), antennas)
+
+        def beam(g, carry, tw=tw, span=span, mw=mw):
+            left = held[tw, :, :, pl.ds(pl.multiple_of(g * tile, tile), tile), :].reshape(parts * tile, antennas)
+            left = jnp.concatenate(
+                [left * (member == c).astype(jnp.float32).astype(jnp.bfloat16) for c in range(group)], axis=1
+            )
+            for k, weight in enumerate((wr, wi)):
+                right = weight[pl.ds(g * group, group), span, :].reshape(group * antennas, beams)
+                product = jnp.dot(left, right, preferred_element_type=jnp.float32)
+                for b in range(beams // lanes):
+                    piece = product[:, b * lanes:(b + 1) * lanes]
+                    at = k * (beams // lanes) + b
+                    if mw == 0:
+                        acc[g, at] = piece
+                    else:
+                        acc[g, at] = acc[g, at] + piece
+            return carry
+
+        lax.fori_loop(0, channels // group, beam, 0)
+
+    for g in range(channels // group):
+        half = parts * group
+        for b in range(beams // lanes):
+            re_re = acc[g, b, pl.ds(0, half, stride=2), :]
+            im_re = acc[g, b, pl.ds(1, half, stride=2), :]
+            re_im = acc[g, beams // lanes + b, pl.ds(0, half, stride=2), :]
+            im_im = acc[g, beams // lanes + b, pl.ds(1, half, stride=2), :]
+            y_re = re_re - im_im
+            y_im = re_im + im_re
+            both = (y_re * y_re + y_im * y_im).reshape(pols, frames, group, lanes)
+            total = both[0]
+            for k in range(1, pols):
+                total = total + both[k]
+            mean = total[0]
+            for k in range(1, frames):
+                mean = mean + total[k]
+            centered = total - (mean * (1.0 / frames))[None]
+            power[:, g * group:(g + 1) * group, b * lanes:(b + 1) * lanes] = centered
+
+    turned = jnp.transpose(power[...].reshape(frames * channels, beams), (1, 0))
+    outgoing[...] = turned.astype(jnp.bfloat16).reshape(outgoing.shape)
+    mine = (w * subs + s) * pols + q
+    slot = pl.ds(pl.multiple_of(mine * lanes, lanes), lanes)
+    shares = []
+    for m in reversed(range(owners)):
+        tw, ts, tq = place(m)
+        source = outgoing.at[tw * subs + ts]
+        target = arrived.at[:, slot]
+        if m == 0:
+            copy = pltpu.make_async_copy(source, target, own_sem.at[1])
+        else:
+            copy = pltpu.make_async_remote_copy(
+                src_ref=source, dst_ref=target, send_sem=psend_sem.at[m], recv_sem=precv_sem.at[m],
+                device_id=ident(m), device_id_type=MESH,
+            )
+        copy.start()
+        shares.append(copy)
+    for m in range(1, owners):
+        copies[m].wait_send()
+    for copy in shares:
+        copy.wait()
+    result = lax.dot_general(
+        arrived[...], hot[...], (((1,), (1,)), ((), ())), preferred_element_type=jnp.float32
+    )
+    out_ref[...] = result * (1.0 / math.sqrt(channel_total))
+
+
+def twiddles(sample_total, channel_total):
+    lanes = 128
+    cycle = sample_total // lanes
+    bins = sample_total // 2 - channel_total + np.arange(channel_total)
+    step = 2.0 * math.pi / sample_total
+    quarter = np.array([0.0, 0.5 * math.pi])
+    inner = (bins[:, None] * np.arange(lanes)[None, :] % sample_total) * step
+    inner = (inner[:, None, :] + quarter[None, :, None]).reshape(2 * channel_total, lanes)
+    outer = (np.arange(cycle)[:, None] * lanes * bins[None, :cycle] % sample_total) * step
+    outer = np.repeat(outer, 2, axis=1)[:, :, None] + np.zeros((1, 1, lanes))
+    factor = 1.0 / math.sqrt(sample_total)
+    return tuple(
+        jnp.asarray(a.astype(np.float32))
+        for a in (np.cos(inner) * factor, np.sin(inner) * factor, np.cos(outer), np.sin(outer))
+    )
+
+
+def window_local(voltages, real_weight, imaginary_weight, delays):
+    wides, subs, pols = (lax.axis_size(a) for a in ("wide", "sub", "pol"))
+    owners = wides * subs * pols
+    _, antennas, fslice, samples = voltages.shape
+    channels, antenna_total, beams = real_weight.shape
+    trials, channel_total = delays.shape
+    frames = subs * fslice
+    beam_local = beams // (wides * subs)
+    parts = subs * pols * fslice
+    lanes = 128
+    tables = twiddles(samples, channel_total)
+    frame_major = jnp.transpose(voltages[0], (1, 0, 2))
+    vmem = pl.BlockSpec(memory_space=pltpu.VMEM)
+    anyspace = pl.BlockSpec(memory_space=pl.ANY)
+    bf16, f32 = jnp.bfloat16, jnp.float32
+    result = pl.pallas_call(
+        functools.partial(window_kernel, (wides, subs, pols, fslice)),
+        out_shape=jax.ShapeDtypeStruct((beam_local, frames * trials), f32),
+        in_specs=[vmem, anyspace, anyspace, vmem, vmem, vmem, vmem, vmem],
+        out_specs=vmem,
+        scratch_shapes=[
+            pltpu.VMEM(real_weight.shape, bf16),
+            pltpu.VMEM(real_weight.shape, bf16),
+            pltpu.VMEM((subs * pols * 2 * channels, samples), bf16),
+            pltpu.VMEM((wides, fslice, subs * pols * 2 * channels, antennas), bf16),
+            pltpu.VMEM((wides, subs * pols, fslice, 2 * channels, antennas), bf16),
+            pltpu.VMEM((channels // 8, 2 * beams // lanes, parts * 16, lanes), f32),
+            pltpu.VMEM((frames, channels, beams), f32),
+            pltpu.VMEM((wides * subs, beam_local, lanes), bf16),
+            pltpu.VMEM((beam_local, owners * lanes), bf16),
+            pltpu.VMEM((frames * trials, owners * lanes), bf16),
+            pltpu.SemaphoreType.DMA((wides, 2)),
+            pltpu.SemaphoreType.DMA((owners,)),
+            pltpu.SemaphoreType.DMA((owners,)),
+            pltpu.SemaphoreType.DMA((2,)),
+            pltpu.SemaphoreType.DMA((owners,)),
+            pltpu.SemaphoreType.DMA((owners,)),
+        ],
+        compiler_params=pltpu.CompilerParams(
+            collective_id=0, has_side_effects=True, vmem_limit_bytes=60 * 1024 * 1024
+        ),
+    )(frame_major, real_weight, imaginary_weight, delays, *tables)
+    return result.reshape(beam_local, frames, trials)
+
+
+def power_of_two(value):
+    return value > 0 and value & (value - 1) == 0
+
+
+def in_one_kernel(voltages, real_weight, delays):
+    wides, subs, pols = (lax.axis_size(a) for a in ("wide", "sub", "pol"))
+    _, antennas, fslice, samples = voltages.shape
+    channels, _, beams = real_weight.shape
+    frames = subs * fslice
+    return (
+        all(power_of_two(v) for v in (wides, subs, pols, frames))
+        and channels % 8 == 0
+        and frames * channels == 128
+        and antennas % 128 == 0
+        and beams % 128 == 0
+        and beams % (wides * subs * 16) == 0
+        and samples % 128 == 0
+        and (subs * pols * channels) % (samples // 128) == 0
+        and delays.shape[1] % 128 == 0
+        and delays.shape[0] % 16 == 0
+        and 4 * real_weight.size <= 36 * 1024 * 1024
+    )
+
+
+def local(voltages, real_weight, imaginary_weight, delays):
+    if in_one_kernel(voltages, real_weight, delays):
+        return window_local(voltages, real_weight, imaginary_weight, delays)
+    return staged_local(voltages, real_weight, imaginary_weight, delays)
+
+
 def solution(mesh):
     placed = (
         P("pol", ("group", "wide"), "sub", None),

time: 324 us -> 47.4 us (0.15)
  local copies, waits for them, and re-layouts: 153 us -> 5.3 us
  other arithmetic: 80.8 us -> 0 us
  matrix products: 62 us -> 0 us
  Pallas kernels: 0 us -> 41.9 us
  starting transfers between devices: 13.3 us -> 0 us
  waiting for transfers between devices: 7.34 us -> 0 us
  blocking collectives: 6.79 us -> 0 us
    reshape x3 -> x1, local copies, waits for them, and re-layouts: 146 us -> 1.48 us  [window_local(): return result.reshape(beam_local, frames, trials)]
    dot_general x10 -> x0, matrix products: 62 us -> none  [the longest x1 42.6 us: local(): jnp.einsum('wsqckaf,ckwaob->cqsfob', voltage_collection, real_form, prefe...]
    another operation x2 -> x0, other arithmetic: 61 us -> none  [the longest x1 44.1 us: local(): real_form = jnp.stack([form_re, form_im], axis=4)]
    pallas_call x0 -> x1, Pallas kernels: none -> 41.9 us  [window_local(): pl.pallas_call(functools.partial(window_kernel, (wides, subs, pols, fslic...]
    neg x1 -> x0, other arithmetic: 14.7 us -> none  [local(): form_re = jnp.stack([real_section, -imaginary_split], axis=1)]
    all_to_all x2 -> x0, starting transfers between devices: 13.3 us -> none  [the longest x1 7.28 us: voltage_turn(): lax.all_to_all(blocks_in, ('wide', 'sub'), split_axis=0, concat_axis=0, t...]
    all_to_all x2 -> x0, waiting for transfers between devices: 7.34 us -> none  [the longest x1 7.34 us: power_turn(): lax.all_to_all(blocks_in, ('wide', 'sub'), split_axis=0, concat_axis=0, t...]
    convert_element_type x3 -> x0, other arithmetic: 5.16 us -> none  [the longest x1 2.71 us: dft_table(): upper = exact.astype(jnp.bfloat16)]
  transfers between devices with their start and end apart: 2 -> 0, of which waited for: 1 -> 0; matrix products, arithmetic and copies ran while one was open for 18% -> 0% of each run, Pallas kernels for 0% -> 0%
where the time goes in v1:
time: 47.4 us; the launch traced here: 47.2 us
  Pallas kernels  41.9 us (88%)
  local copies, waits for them, and re-layouts  5.3 us (11%)
    pallas_call x1, Pallas kernels, window_local(): pl.pallas_call(functools.partial(window_kernel, (wides, subs, pols, fslic...  41.9 us
    unnamed x1, local copies, waits for them, and re-layouts  3.82 us
    reshape x1, local copies, waits for them, and re-layouts, window_local(): return result.reshape(beam_local, frames, trials)  1.48 us

profile of v1, /device:TPU:0, one launch (start us, length us, event | category | flops | bytes accessed | tf_op | source)
XLA Modules:
  0.0 47.2 jit_solution(13122771906871191084)
XLA Ops:
  0.0 3.8 %copy.11 = bf16[1,256,2,2048]{3,1,2,0:T(8,128)(2,1)} copy(bf16[1,256,2,2048]{3,2,1,0:T(2,128)(2,1)} %param.8) | data formatting | bytes 4194304 | tf_op args[0]
  3.8 41.9 %shard_map.82 = f32[32,256]{1,0:T(8,128)} custom-call(bf16[2,256,2048]{2,1,0:T(8,128)(2,1)} %bitcast.5, bf16[32,1024,256]{2,1,0:T(8,128)(2,1)} %wr_hbm.1, bf16[32,1024,256]{2,1,0:T(8,128)(2,1)} %wi_hbm.1, s32[64,512]{1,0:T(8,128)} %d_ref.1, f32[1024,128]{1,0:T(8,128)} %constant.8.clone.cb_ref, f32[1024,128]{1,0:T(8,128)} %constant.9.clone.sb_ref, ...), custom_call_target="tpu_custom_call" | custom-call | tf_op jit(solution)/shard_map/pallas_call | solution.py:362
  45.7 1.5 %reshape.3 = f32[32,4,64]{2,1,0:T(4,128)} reshape(f32[32,256]{1,0:T(8,128)} %shard_map.82) | data formatting | bytes 65536 | tf_op jit(solution)/shard_map/reshape | solution.py:389

commit v2 on v1

--- a/solution.py
+++ b/solution.py
@@ -153,7 +153,7 @@
 def window_kernel(
     dims, v_ref, wr_hbm, wi_hbm, d_ref, cb_ref, sb_ref, ca_ref, sa_ref, out_ref,
     wr, wi, table, sent, held, acc, power, outgoing, arrived, hot,
-    w_sem, send_sem, recv_sem, own_sem, psend_sem, precv_sem,
+    w_sem, send_sem, recv_sem, own_sem, psend_sem, precv_sem, fsend_sem, frecv_sem,
 ):
     wides, subs, pols, fslice = dims
     per_wide = subs * pols
@@ -194,42 +194,69 @@
 
     chunk = per_wide * rows
     cycle = ca_ref.shape[1]
+    tile = 16
+    group = tile // 2
+    groups = channels // group
+    last = wides // 2
     copies = [None] * owners
+    fine = {}
+
+    def spectra(base, count, j, start):
+        def fill(n1, carry):
+            cos_in = cb_ref[pl.ds(base, count), :].reshape(count // cycle, cycle, lanes)
+            sin_in = sb_ref[pl.ds(base, count), :].reshape(count // cycle, cycle, lanes)
+            value = cos_in * ca_ref[n1][None] - sin_in * sa_ref[n1][None]
+            at = pl.ds(pl.multiple_of(n1 * lanes, lanes), lanes)
+            table[:count, at] = value.reshape(count, lanes).astype(jnp.bfloat16)
+            return carry
+
+        lax.fori_loop(0, samples // lanes, fill, 0)
+        for f in range(fslice):
+            spectrum = lax.dot_general(
+                table[:count, :], v_ref[f], (((1,), (1,)), ((), ())), preferred_element_type=jnp.float32
+            )
+            sent[j, f, start:start + count, :] = spectrum.astype(jnp.bfloat16)
+
+    def ship(m, source, target, send, recv):
+        if m == 0:
+            copy = pltpu.make_async_copy(source, target, recv)
+        else:
+            copy = pltpu.make_async_remote_copy(
+                src_ref=source, dst_ref=target, send_sem=send, recv_sem=recv,
+                device_id=ident(m), device_id_type=MESH,
+            )
+        copy.start()
+        return copy
+
     for j in range(wides):
         mw = wides - 1 - j
         tw = flip(w, mw, wides)
-        base = pl.multiple_of(tw * chunk, chunk)
-
-        def fill(n1, carry, base=base):
-            cos_in = cb_ref[pl.ds(base, chunk), :].reshape(chunk // cycle, cycle, lanes)
-            sin_in = sb_ref[pl.ds(base, chunk), :].reshape(chunk // cycle, cycle, lanes)
-            value = cos_in * ca_ref[n1][None] - sin_in * sa_ref[n1][None]
-            table[:, pl.ds(pl.multiple_of(n1 * lanes, lanes), lanes)] = value.reshape(chunk, lanes).astype(jnp.bfloat16)
-            return carry
-
-        lax.fori_loop(0, samples // lanes, fill, 0)
-        for f in range(fslice):
-            spectrum = lax.dot_general(
-                table[...], v_ref[f], (((1,), (1,)), ((), ())), preferred_element_type=jnp.float32
-            )
-            sent[j, f] = spectrum.astype(jnp.bfloat16)
         if j == 0:
-            pl.semaphore_wait(barrier, owners - 1)
-        for r in reversed(range(per_wide)):
-            m = mw * per_wide + r
-            tw, ts, tq = place(m)
-            part = pl.ds(pl.multiple_of((ts * pols + tq) * rows, rows), rows)
-            source = sent.at[j, :, part, :]
-            target = held.at[w, q * subs + s]
-            if m == 0:
-                copy = pltpu.make_async_copy(source, target, own_sem.at[0])
-            else:
-                copy = pltpu.make_async_remote_copy(
-                    src_ref=source, dst_ref=target, send_sem=send_sem.at[m], recv_sem=recv_sem.at[m],
-                    device_id=ident(m), device_id_type=MESH,
-                )
-            copy.start()
-            copies[m] = copy
+            half = pols * rows
+            for h, ms in enumerate(reversed(range(subs))):
+                ts = flip(s, ms, subs)
+                spectra(pl.multiple_of((tw * subs + ts) * half, half), half, j, h * half)
+                if h == 0:
+                    pl.semaphore_wait(barrier, owners - 1)
+                for mq in reversed(range(pols)):
+                    m = mw * per_wide + ms * pols + mq
+                    tq = flip(q, mq, pols)
+                    part = pl.ds(pl.multiple_of(h * half + tq * rows, rows), rows)
+                    copies[m] = ship(m, sent.at[j, :, part, :], held.at[w, q * subs + s], send_sem.at[m], recv_sem.at[m])
+        else:
+            spectra(pl.multiple_of(tw * chunk, chunk), chunk, j, 0)
+            for g in range(groups if mw == last else 1):
+                for r in reversed(range(per_wide)):
+                    m = mw * per_wide + r
+                    _, ts, tq = place(m)
+                    if mw == last:
+                        part = pl.ds(pl.multiple_of((ts * pols + tq) * rows + g * tile, tile), tile)
+                        target = held.at[w, q * subs + s, :, g * tile:(g + 1) * tile, :]
+                        fine[g, r] = ship(m, sent.at[j, :, part, :], target, fsend_sem.at[g, r], frecv_sem.at[g, r])
+                    else:
+                        part = pl.ds(pl.multiple_of((ts * pols + tq) * rows, rows), rows)
+                        recv = own_sem.at[0] if m == 0 else recv_sem.at[m]
+                        copies[m] = ship(m, sent.at[j, :, part, :], held.at[w, q * subs + s], send_sem.at[m], recv)
 
     per_tile = lanes // channels
     lane = lax.broadcasted_iota(jnp.int32, (lanes, lanes), 1)
@@ -245,48 +272,34 @@
                 wanted = ((frame_lane - n) & (frames - 1)).astype(jnp.float32)
                 hot[n * trials:(n + 1) * trials, at:at + lanes] = (wide_delay == wanted).astype(jnp.float32).astype(jnp.bfloat16)
 
-    tile = 16
-    group = tile // 2
     parts = per_wide * fslice
     member = lax.broadcasted_iota(jnp.int32, (parts * tile, antennas), 0) // 2 % group
-    for mw in range(wides):
+
+    def beam(g, mw):
         tw = flip(w, mw, wides)
-        for copy in loads[mw]:
-            copy.wait()
-        for r in range(per_wide):
-            m = mw * per_wide + r
-            if m == 0:
-                copies[0].wait()
-            else:
-                copies[m].wait_recv()
         span = pl.ds(pl.multiple_of(tw * antennas, antennas), antennas)
-
-        def beam(g, carry, tw=tw, span=span, mw=mw):
-            left = held[tw, :, :, pl.ds(pl.multiple_of(g * tile, tile), tile), :].reshape(parts * tile, antennas)
-            left = jnp.concatenate(
-                [left * (member == c).astype(jnp.float32).astype(jnp.bfloat16) for c in range(group)], axis=1
-            )
-            for k, weight in enumerate((wr, wi)):
-                right = weight[pl.ds(g * group, group), span, :].reshape(group * antennas, beams)
-                product = jnp.dot(left, right, preferred_element_type=jnp.float32)
-                for b in range(beams // lanes):
-                    piece = product[:, b * lanes:(b + 1) * lanes]
-                    at = k * (beams // lanes) + b
-                    if mw == 0:
-                        acc[g, at] = piece
-                    else:
-                        acc[g, at] = acc[g, at] + piece
-            return carry
-
-        lax.fori_loop(0, channels // group, beam, 0)
-
-    for g in range(channels // group):
-        half = parts * group
+        left = held[tw, :, :, pl.ds(pl.multiple_of(g * tile, tile), tile), :].reshape(parts * tile, antennas)
+        left = jnp.concatenate(
+            [left * (member == c).astype(jnp.float32).astype(jnp.bfloat16) for c in range(group)], axis=1
+        )
+        for k, weight in enumerate((wr, wi)):
+            right = weight[pl.ds(g * group, group), span, :].reshape(group * antennas, beams)
+            product = jnp.dot(left, right, preferred_element_type=jnp.float32)
+            for b in range(beams // lanes):
+                piece = product[:, b * lanes:(b + 1) * lanes]
+                at = k * (beams // lanes) + b
+                if mw == 0:
+                    acc[g, at] = piece
+                else:
+                    acc[g, at] = acc[g, at] + piece
+
+    def strength(g):
+        count = parts * group
         for b in range(beams // lanes):
-            re_re = acc[g, b, pl.ds(0, half, stride=2), :]
-            im_re = acc[g, b, pl.ds(1, half, stride=2), :]
-            re_im = acc[g, beams // lanes + b, pl.ds(0, half, stride=2), :]
-            im_im = acc[g, beams // lanes + b, pl.ds(1, half, stride=2), :]
+            re_re = acc[g, b, pl.ds(0, count, stride=2), :]
+            im_re = acc[g, b, pl.ds(1, count, stride=2), :]
+            re_im = acc[g, beams // lanes + b, pl.ds(0, count, stride=2), :]
+            im_im = acc[g, beams // lanes + b, pl.ds(1, count, stride=2), :]
             y_re = re_re - im_im
             y_im = re_im + im_re
             both = (y_re * y_re + y_im * y_im).reshape(pols, frames, group, lanes)
@@ -298,6 +311,29 @@
                 mean = mean + total[k]
             centered = total - (mean * (1.0 / frames))[None]
             power[:, g * group:(g + 1) * group, b * lanes:(b + 1) * lanes] = centered
+
+    for mw in [0] + [k for k in reversed(range(1, wides)) if k != last]:
+        for copy in loads[mw]:
+            copy.wait()
+        for r in range(per_wide):
+            m = mw * per_wide + r
+            if m == 0:
+                copies[0].wait()
+            else:
+                copies[m].wait_recv()
+
+        def whole(g, carry, mw=mw):
+            beam(g, mw)
+            return carry
+
+        lax.fori_loop(0, groups, whole, 0)
+    for copy in loads[last]:
+        copy.wait()
+    for g in range(groups):
+        for r in range(per_wide):
+            fine[g, r].wait_recv()
+        beam(g, last)
+        strength(g)
 
     turned = jnp.transpose(power[...].reshape(frames * channels, beams), (1, 0))
     outgoing[...] = turned.astype(jnp.bfloat16).reshape(outgoing.shape)
@@ -317,14 +353,16 @@
             )
         copy.start()
         shares.append(copy)
-    for m in range(1, owners):
-        copies[m].wait_send()
+    for copy in [c for c in copies[1:] if c is not None] + list(fine.values()):
+        copy.wait_send()
     for copy in shares:
         copy.wait()
     result = lax.dot_general(
         arrived[...], hot[...], (((1,), (1,)), ((), ())), preferred_element_type=jnp.float32
     )
-    out_ref[...] = result * (1.0 / math.sqrt(channel_total))
+    result = result * (1.0 / math.sqrt(channel_total))
+    for n in range(frames):
+        out_ref[:, n, :] = result[:, n * trials:(n + 1) * trials]
 
 
 def twiddles(sample_total, channel_total):
@@ -361,7 +399,7 @@
     bf16, f32 = jnp.bfloat16, jnp.float32
     result = pl.pallas_call(
         functools.partial(window_kernel, (wides, subs, pols, fslice)),
-        out_shape=jax.ShapeDtypeStruct((beam_local, frames * trials), f32),
+        out_shape=jax.ShapeDtypeStruct((beam_local, frames, trials), f32),
         in_specs=[vmem, anyspace, anyspace, vmem, vmem, vmem, vmem, vmem],
         out_specs=vmem,
         scratch_shapes=[
@@ -381,12 +419,14 @@
             pltpu.SemaphoreType.DMA((2,)),
             pltpu.SemaphoreType.DMA((owners,)),
             pltpu.SemaphoreType.DMA((owners,)),
+            pltpu.SemaphoreType.DMA((channels // 8, subs * pols)),
+            pltpu.SemaphoreType.DMA((channels // 8, subs * pols)),
         ],
         compiler_params=pltpu.CompilerParams(
             collective_id=0, has_side_effects=True, vmem_limit_bytes=60 * 1024 * 1024
         ),
     )(frame_major, real_weight, imaginary_weight, delays, *tables)
-    return result.reshape(beam_local, frames, trials)
+    return result
 
 
 def power_of_two(value):
@@ -400,13 +440,14 @@
     frames = subs * fslice
     return (
         all(power_of_two(v) for v in (wides, subs, pols, frames))
+        and wides > 1
+        and (pols * 2 * channels) % (samples // 128 * 2) == 0
         and channels % 8 == 0
         and frames * channels == 128
         and antennas % 128 == 0
         and beams % 128 == 0
         and beams % (wides * subs * 16) == 0
         and samples % 128 == 0
-        and (subs * pols * channels) % (samples // 128) == 0
         and delays.shape[1] % 128 == 0
         and delays.shape[0] % 16 == 0
         and 4 * real_weight.size <= 36 * 1024 * 1024

time: 47.4 us -> 45.7 us (0.964)
  Pallas kernels: 41.9 us -> 40.2 us
    pallas_call x1, Pallas kernels: 41.9 us -> 40.2 us  [window_local(): pl.pallas_call(functools.partial(window_kernel, (wides, subs, pols, fslic...]
    reshape x1 -> x0, local copies, waits for them, and re-layouts: 1.48 us -> none  [window_local(): return result.reshape(beam_local, frames, trials)]
    unnamed x1 -> x2, local copies, waits for them, and re-layouts: 3.82 us -> 5.29 us
where the time goes in v2:
time: 45.7 us; the launch traced here: 45.5 us
  Pallas kernels  40.2 us (88%)
  local copies, waits for them, and re-layouts  5.29 us (12%)
    pallas_call x1, Pallas kernels, window_local(): pl.pallas_call(functools.partial(window_kernel, (wides, subs, pols, fslic...  40.2 us
    unnamed x2, local copies, waits for them, and re-layouts  5.29 us

profile of v2, /device:TPU:0, one launch (start us, length us, event | category | flops | bytes accessed | tf_op | source)
XLA Modules:
  0.0 45.5 jit_solution(2489009848867566231)
XLA Ops:
  0.0 3.8 %copy.11 = bf16[1,256,2,2048]{3,1,2,0:T(8,128)(2,1)} copy(bf16[1,256,2,2048]{3,2,1,0:T(2,128)(2,1)} %param.8) | data formatting | bytes 4194304 | tf_op args[0]
  3.8 40.2 %shard_map.82 = f32[32,4,64]{2,1,0:T(4,128)} custom-call(bf16[2,256,2048]{2,1,0:T(8,128)(2,1)} %bitcast.5, bf16[32,1024,256]{2,1,0:T(8,128)(2,1)} %wr_hbm.1, bf16[32,1024,256]{2,1,0:T(8,128)(2,1)} %wi_hbm.1, s32[64,512]{1,0:T(8,128)} %d_ref.1, f32[1024,128]{1,0:T(8,128)} %constant.8.clone.cb_ref, f32[1024,128]{1,0:T(8,128)} %constant.9.clone.sb_ref, ...), custom_call_target="tpu_custom_call" | custom-call | tf_op jit(solution)/shard_map/pallas_call | solution.py:400
  44.1 1.5 %copy.13 = f32[32,4,64]{2,1,0:T(4,128)} copy(f32[32,4,64]{2,1,0:T(4,128)} %shard_map.82) | data formatting | bytes 65536

commit v3 on v2

--- a/solution.py
+++ b/solution.py
@@ -151,8 +151,8 @@
 
 
 def window_kernel(
-    dims, v_ref, wr_hbm, wi_hbm, d_ref, cb_ref, sb_ref, ca_ref, sa_ref, out_ref,
-    wr, wi, table, sent, held, acc, power, outgoing, arrived, hot,
+    dims, raw_ref, wr_hbm, wi_hbm, d_ref, cb_ref, sb_ref, ca_ref, sa_ref, out_ref,
+    wr, wi, v_ref, table, sent, held, acc, power, outgoing, arrived, hot,
     w_sem, send_sem, recv_sem, own_sem, psend_sem, precv_sem, fsend_sem, frecv_sem,
 ):
     wides, subs, pols, fslice = dims
@@ -192,6 +192,13 @@
             pair.append(copy)
         loads.append(pair)
 
+    def part_frames(k, carry):
+        at = pl.ds(pl.multiple_of(k * 16, 16), 16)
+        for f in range(fslice):
+            v_ref[f, at, :] = raw_ref[at, f, :]
+        return carry
+
+    lax.fori_loop(0, antennas // 16, part_frames, 0)
     chunk = per_wide * rows
     cycle = ca_ref.shape[1]
     tile = 16
@@ -393,7 +400,6 @@
     parts = subs * pols * fslice
     lanes = 128
     tables = twiddles(samples, channel_total)
-    frame_major = jnp.transpose(voltages[0], (1, 0, 2))
     vmem = pl.BlockSpec(memory_space=pltpu.VMEM)
     anyspace = pl.BlockSpec(memory_space=pl.ANY)
     bf16, f32 = jnp.bfloat16, jnp.float32
@@ -405,6 +411,7 @@
         scratch_shapes=[
             pltpu.VMEM(real_weight.shape, bf16),
             pltpu.VMEM(real_weight.shape, bf16),
+            pltpu.VMEM((fslice, antennas, samples), bf16),
             pltpu.VMEM((subs * pols * 2 * channels, samples), bf16),
             pltpu.VMEM((wides, fslice, subs * pols * 2 * channels, antennas), bf16),
             pltpu.VMEM((wides, subs * pols, fslice, 2 * channels, antennas), bf16),
@@ -425,7 +432,7 @@
         compiler_params=pltpu.CompilerParams(
             collective_id=0, has_side_effects=True, vmem_limit_bytes=60 * 1024 * 1024
         ),
-    )(frame_major, real_weight, imaginary_weight, delays, *tables)
+    )(voltages[0], real_weight, imaginary_weight, delays, *tables)
     return result
 
 

time: 45.7 us -> 43.9 us (0.961)
  local copies, waits for them, and re-layouts: 5.29 us -> 1.47 us
  Pallas kernels: 40.2 us -> 42.3 us
    unnamed x2 -> x1, local copies, waits for them, and re-layouts: 5.29 us -> 1.47 us
    pallas_call x1, Pallas kernels: 40.2 us -> 42.3 us  [window_local(): pl.pallas_call(functools.partial(window_kernel, (wides, subs, pols, fslic...]
where the time goes in v3:
time: 43.9 us; the launch traced here: 43.7 us
  Pallas kernels  42.3 us (96%)
  local copies, waits for them, and re-layouts  1.47 us (3%)
    pallas_call x1, Pallas kernels, window_local(): pl.pallas_call(functools.partial(window_kernel, (wides, subs, pols, fslic...  42.3 us
    unnamed x1, local copies, waits for them, and re-layouts  1.47 us

profile of v3, /device:TPU:0, one launch (start us, length us, event | category | flops | bytes accessed | tf_op | source)
XLA Modules:
  0.0 43.7 jit_solution(17664930957444548595)
XLA Ops:
  0.0 42.3 %shard_map.82 = f32[32,4,64]{2,1,0:T(4,128)} custom-call(bf16[256,2,2048]{2,1,0:T(2,128)(2,1)} %bitcast.1, bf16[32,1024,256]{2,1,0:T(8,128)(2,1)} %wr_hbm.1, bf16[32,1024,256]{2,1,0:T(8,128)(2,1)} %wi_hbm.1, s32[64,512]{1,0:T(8,128)} %d_ref.1, f32[1024,128]{1,0:T(8,128)} %constant.8.clone.cb_ref, f32[1024,128]{1,0:T(8,128)} %constant.9.clone.sb_ref, ...), custom_call_target="tpu_custom_call" | custom-call | tf_op jit(solution)/shard_map/pallas_call | solution.py:406
  42.3 1.5 %copy.10 = f32[32,4,64]{2,1,0:T(4,128)} copy(f32[32,4,64]{2,1,0:T(4,128)} %shard_map.82) | data formatting | bytes 65536
